TPU v7x, 32 devices: a whole 2x2x4 slice. The times are simulated.
32 devices in a mesh: snap: 2 (over y), row: 4 (over z), col: 4 (over x, core).
Axes of the slice: x: 2, y: 2, z: 4, core: 2. Of those that a mesh axis runs over, the one named last changes fastest.
Arguments:
- orbitals: float32 [12288, 768], P(('snap', 'row', 'col')), parts along dimension 0, may hold values from -6 to 6
- screened: float32 [6, 6144, 6144], P('snap', 'row', 'col'), parts along dimension 0, may hold values from -0.0029296875 to 0.0029296875
- green_weight: float32 [6, 768], P('snap'), parts along dimension 0, may hold values from 0.05 to 1
- time_weight: float32 [3], replicated, may hold values from 0.3 to 1
Outputs:
- updated: float32 [12288, 768], P(('snap', 'row', 'col')), parts along dimension 0
There are 2 independent parts, one for each index of `snap`. A program takes and returns all parts, laid end to end along the dimension named above; an argument that names none is the same for every part. Nothing has to cross between parts.
All inputs are finite; a program needn't handle non-finite values.
Results may differ from a plain program's by a relative error of at most 0.00013.
Values sent between devices are 32-bit elements; how exact they have to be, the bound alone decides.
A program may use at most 128 MiB of HBM per device.

v0:
```python
import jax
import jax.numpy as jnp
from jax import lax
from jax.sharding import PartitionSpec as P

TIMES = 3
PASSES = 2


def from_root(block, axis, owner):
    block = jnp.where(lax.axis_index(axis) == owner, block, jnp.zeros_like(block))
    return lax.psum(block, axis)


def gather_rows(shard):
    return lax.all_gather(shard, "col", axis=0, tiled=True)


def scatter_rows(partial_value):
    return lax.psum_scatter(partial_value, "col", scatter_dimension=0, tiled=True)


def body(orbitals, screened, green_weight, time_weight):
    n_row = lax.axis_size("row")
    n_col = lax.axis_size("col")
    factor = n_col // n_row
    col_width = screened.shape[2]
    col_index = lax.axis_index("col")
    root = col_index // factor
    offset = col_index % factor * col_width
    own = orbitals
    rows = gather_rows(own)
    for step in range(PASSES):
        piece = lax.dynamic_slice_in_dim(rows, offset, col_width, 0)
        columns = from_root(piece, "row", root)
        partial_value = jnp.zeros(rows.shape, jnp.float32)
        for t in range(TIMES):
            green = lax.dot_general(
                rows * green_weight[t],
                columns,
                (((1,), (1,)), ((), ())),
                precision=lax.Precision.HIGHEST,
                preferred_element_type=jnp.float32,
            )
            applied = jnp.dot(
                green * screened[t],
                columns,
                precision=lax.Precision.HIGHEST,
                preferred_element_type=jnp.float32,
            )
            partial_value = partial_value + time_weight[t] * applied
        final = step == PASSES - 1
        own = own - scatter_rows(partial_value)
        if not final:
            rows = gather_rows(own)
    return own


def solution(mesh):
    in_specs = (P(("snap", "row", "col"), None), P("snap", "row", "col"), P("snap", None), P())
    out_specs = P(("snap", "row", "col"), None)
    return jax.shard_map(body, mesh=mesh, in_specs=in_specs, out_specs=out_specs, check_vma=False)
```

profile of v0, /device:TPU:0, one launch (start us, length us, event | category | flops | bytes accessed | tf_op | source)
XLA Modules:
  0.0 877.8 jit_solution(2341078948588468849)
XLA Ops:
  6.5 0.0 all-gather.3.cloned.1.call-start
  6.5 0.7 all-gather.3.cloned.1.call-update
  7.3 0.0 all-reduce.3.cloned.1.call-start
  7.3 41.8 %all-gather.3.cloned.1.call-done = f32[1536,768]{1,0:T(8,128)} async-done(((f32[384,768]{1,0:T(8,128)}), f32[1536,768]{1,0:T(8,128)}) %all-gather.3.cloned.1.call-update) | async-done | bytes 4718608 | tf_op jit(solution)/shard_map/all_gather | solution.py:16
  49.1 4.8 broadcast_select_fusion.1
  53.9 0.0 all-reduce.3.cloned.1.call-update
  53.9 0.0 reduce-scatter.3.cloned.1.call-start
  53.9 0.6 copy-done.4
  54.5 0.6 fusion.12
  55.2 0.0 copy-done.3
  55.2 170.7 %all-reduce.3.cloned.1.call-done = f32[1536,768]{1,0:T(8,128)} async-done(((f32[1536,768]{1,0:T(8,128)}), f32[1536,768]{1,0:T(8,128)}) %all-reduce.3.cloned.1.call-update) | async-done | bytes 4718608 | tf_op jit(solution)/shard_map/psum | solution.py:12
  225.9 28.3 %convolution_multiply_fusion.4 = f32[1536,1536]{1,0:T(8,128)} fusion(f32[1536,768]{1,0:T(8,128)} %all-reduce.3.cloned.1.call-done, f32[3,1536,1536]{2,1,0:T(8,128)} %param.5, f32[1536,768]{1,0:T(8,128)} %all-gather.3.cloned.1.call-done, f32[768]{0:T(1024)S(1)} %get-tuple-element.7), kind=kOutput, calls=%fused_computation.4 | convolution fusion | flops 21746810880 | bytes 28314624 | tf_op jit(solution)/shard_map/dot_general | solution.py:38
  254.2 28.0 %fusion.14 = f32[1536,768]{1,0:T(8,128)} fusion(f32[1536,1536]{1,0:T(8,128)} %convolution_multiply_fusion.4, f32[1536,768]{1,0:T(8,128)} %all-reduce.3.cloned.1.call-done), kind=kOutput, calls=%fused_computation.27 | convolution fusion | flops 21743271936 | bytes 18874368 | tf_op jit(solution)/shard_map/dot_general | solution.py:45
  282.2 0.0 slice-done.7
  282.2 0.0 slice-done
  282.2 0.0 slice-done.1
  282.2 0.0 slice-done.2
  282.2 0.0 slice-done.3
  282.2 0.0 slice-done.8
  282.2 0.0 slice-done.4
  282.2 0.0 slice-done.5
  282.2 26.8 %convolution_multiply_fusion.5 = f32[1536,1536]{1,0:T(8,128)} fusion(f32[1536,768]{1,0:T(8,128)} %all-reduce.3.cloned.1.call-done, f32[3,1536,1536]{2,1,0:T(8,128)S(1)} %bitcast.31, f32[1536,768]{1,0:T(8,128)S(1)} %bitcast.33, f32[768]{0:T(1024)S(1)} %get-tuple-element.6), kind=kOutput, calls=%fused_computation.5 | convolution fusion | flops 21746810880 | bytes 28314624 | tf_op jit(solution)/shard_map/dot_general | solution.py:38
  309.0 27.7 %fusion.13 = f32[1536,768]{1,0:T(8,128)} fusion(f32[1536,1536]{1,0:T(8,128)} %convolution_multiply_fusion.5, f32[1536,768]{1,0:T(8,128)} %all-reduce.3.cloned.1.call-done), kind=kOutput, calls=%fused_computation.26 | convolution fusion | flops 21743271936 | bytes 18874368 | tf_op jit(solution)/shard_map/dot_general | solution.py:45
  336.8 27.0 %convolution_multiply_fusion.3 = f32[1536,1536]{1,0:T(8,128)} fusion(f32[1536,768]{1,0:T(8,128)} %all-reduce.3.cloned.1.call-done, f32[3,1536,1536]{2,1,0:T(8,128)S(1)} %bitcast.31, f32[1536,768]{1,0:T(8,128)S(1)} %bitcast.33, f32[768]{0:T(1024)S(1)} %get-tuple-element.5), kind=kOutput, calls=%fused_computation.3 | convolution fusion | flops 21746810880 | bytes 28314624 | tf_op jit(solution)/shard_map/dot_general | solution.py:38
  363.8 31.6 %multiply_add_fusion.1 = f32[1536,768]{1,0:T(8,128)} fusion(f32[1536,768]{1,0:T(8,128)} %fusion.14, f32[1536,768]{1,0:T(8,128)} %fusion.13, f32[1536,1536]{1,0:T(8,128)} %convolution_multiply_fusion.3, f32[1536,768]{1,0:T(8,128)} %all-reduce.3.cloned.1.call-done, f32[]{:T(128)} %bitcast.4, f32[]{:T(128)} %bitcast.2, f32[]{:T(128)} %bitcast), kind=kOutput, calls=%fused_computation.10 | convolution fusion | flops 21749170176 | bytes 28311564 | tf_op jit(solution)/shard_map/dot_general | solution.py:45
  395.4 0.0 copy-start.2
  395.4 0.0 reduce-scatter.3.cloned.1.call-update
  395.4 0.0 all-gather.5.cloned.1.call-start
  395.5 47.0 %reduce-scatter.3.cloned.1.call-done = f32[384,768]{1,0:T(8,128)} async-done(((f32[1536,768]{1,0:T(8,128)}), f32[384,768]{1,0:T(8,128)}) %reduce-scatter.3.cloned.1.call-update) | async-done | bytes 1179664 | tf_op jit(solution)/shard_map/reduce_scatter | solution.py:20
  442.5 2.4 sub.8
  444.9 0.0 all-gather.5.cloned.1.call-update
  445.0 0.0 all-reduce.5.cloned.1.call-start
  445.0 37.5 %all-gather.5.cloned.1.call-done = f32[1536,768]{1,0:T(8,128)} async-done(((f32[384,768]{1,0:T(8,128)}), f32[1536,768]{1,0:T(8,128)}) %all-gather.5.cloned.1.call-update) | async-done | bytes 4718608 | tf_op jit(solution)/shard_map/all_gather | solution.py:16
  482.5 4.8 broadcast_select_fusion
  487.4 0.0 all-reduce.5.cloned.1.call-update
  487.4 0.0 reduce-scatter.5.cloned.1.call-start
  487.5 171.9 %all-reduce.5.cloned.1.call-done = f32[1536,768]{1,0:T(8,128)} async-done(((f32[1536,768]{1,0:T(8,128)}), f32[1536,768]{1,0:T(8,128)}) %all-reduce.5.cloned.1.call-update) | async-done | bytes 4718608 | tf_op jit(solution)/shard_map/psum | solution.py:12
  659.4 27.4 %convolution_multiply_fusion.1 = f32[1536,1536]{1,0:T(8,128)S(1)} fusion(f32[1536,768]{1,0:T(8,128)} %all-reduce.5.cloned.1.call-done, f32[3,1536,1536]{2,1,0:T(8,128)} %param.5, f32[1536,768]{1,0:T(8,128)} %all-gather.5.cloned.1.call-done, f32[768]{0:T(1024)S(1)} %get-tuple-element.7), kind=kOutput, calls=%fused_computation.1 | convolution fusion | flops 21746810880 | bytes 28314624 | tf_op jit(solution)/shard_map/dot_general | solution.py:38
  686.8 0.0 copy-done
  686.8 0.0 slice-start.10
  686.8 27.3 %convolution_multiply_fusion.2 = f32[1536,1536]{1,0:T(8,128)} fusion(f32[1536,768]{1,0:T(8,128)S(1)} %copy-done, f32[3,1536,1536]{2,1,0:T(8,128)} %param.5, f32[1536,768]{1,0:T(8,128)} %all-gather.5.cloned.1.call-done, f32[768]{0:T(1024)S(1)} %get-tuple-element.6), kind=kOutput, calls=%fused_computation.2 | convolution fusion | flops 21746810880 | bytes 28314624 | tf_op jit(solution)/shard_map/dot_general | solution.py:38
  714.2 28.4 %convolution_multiply_fusion = f32[1536,1536]{1,0:T(8,128)S(1)} fusion(f32[1536,768]{1,0:T(8,128)S(1)} %copy-done, f32[3,1536,1536]{2,1,0:T(8,128)} %param.5, f32[1536,768]{1,0:T(8,128)S(1)} %bitcast.35, f32[768]{0:T(1024)S(1)} %get-tuple-element.5), kind=kOutput, calls=%fused_computation | convolution fusion | flops 21746810880 | bytes 28314624 | tf_op jit(solution)/shard_map/dot_general | solution.py:38
  742.6 23.3 %fusion.16 = f32[1536,768]{1,0:T(8,128)S(1)} fusion(f32[1536,1536]{1,0:T(8,128)S(1)} %convolution_multiply_fusion.1, f32[1536,768]{1,0:T(8,128)S(1)} %copy-done), kind=kOutput, calls=%fused_computation.29 | convolution fusion | flops 21743271936 | bytes 18874368 | tf_op jit(solution)/shard_map/dot_general | solution.py:45
  765.9 28.4 %fusion.15 = f32[1536,768]{1,0:T(8,128)S(1)} fusion(f32[1536,1536]{1,0:T(8,128)} %convolution_multiply_fusion.2, f32[1536,768]{1,0:T(8,128)S(1)} %copy-done), kind=kOutput, calls=%fused_computation.28 | convolution fusion | flops 21743271936 | bytes 18874368 | tf_op jit(solution)/shard_map/dot_general | solution.py:45
  794.2 27.0 %multiply_add_fusion = f32[1536,768]{1,0:T(8,128)} fusion(f32[1536,768]{1,0:T(8,128)S(1)} %fusion.16, f32[1536,768]{1,0:T(8,128)S(1)} %fusion.15, f32[1536,1536]{1,0:T(8,128)S(1)} %convolution_multiply_fusion, f32[1536,768]{1,0:T(8,128)S(1)} %copy-done, f32[]{:T(128)} %bitcast.4, f32[]{:T(128)} %bitcast.2, f32[]{:T(128)} %bitcast), kind=kOutput, calls=%fused_computation.6 | convolution fusion | flops 21749170176 | bytes 28311564 | tf_op jit(solution)/shard_map/dot_general | solution.py:45
  821.2 0.0 reduce-scatter.5.cloned.1.call-update
  821.2 47.1 %reduce-scatter.5.cloned.1.call-done = f32[384,768]{1,0:T(8,128)} async-done(((f32[1536,768]{1,0:T(8,128)}), f32[384,768]{1,0:T(8,128)}) %reduce-scatter.5.cloned.1.call-update) | async-done | bytes 1179664 | tf_op jit(solution)/shard_map/reduce_scatter | solution.py:20
  868.3 2.4 sub.9
  (23 shorter events, 0.1 us)
Async XLA Ops:
  6.5 42.5 %all-gather.3.cloned.1.call-start = ((), (), s32[]{:S(2)}) async-start(), calls=%async_computation.2 | async-start | bytes 5898240 | tf_op jit(solution)/shard_map/all_gather | solution.py:16
  7.3 218.6 %all-reduce.3.cloned.1.call-start = ((), (), s32[]{:S(2)}) async-start(), calls=%async_computation.3 | async-start | bytes 9437184 | tf_op jit(solution)/shard_map/psum | solution.py:12
  53.9 0.7 copy-start.4
  53.9 1.3 copy-start.3
  53.9 228.3 %slice-start.7 = ((s8[4718592]{0:T(1024)(128)(4,1)}), s8[524288]{0:T(1024)(128)(4,1)S(1)}, s32[]{:S(2)}) async-start(s8[4718592]{0:T(1024)(128)(4,1)} %bitcast.32), calls=%async_computation.15 | async-start | bytes 1048576
  53.9 388.6 %reduce-scatter.3.cloned.1.call-start = ((), (), s32[]{:S(2)}) async-start(), calls=%async_computation.4 | async-start | bytes 5898240 | tf_op jit(solution)/shard_map/reduce_scatter | solution.py:20
  225.9 56.3 %slice-start = ((s8[28311552]{0:T(1024)(128)(4,1)}), s8[4194304]{0:T(1024)(128)(4,1)S(1)}, s32[]{:S(2)}) async-start(s8[28311552]{0:T(1024)(128)(4,1)} %bitcast.30), calls=%async_computation.8 | async-start | bytes 8388608
  225.9 56.3 %slice-start.1 = ((s8[28311552]{0:T(1024)(128)(4,1)}), s8[4194304]{0:T(1024)(128)(4,1)S(1)}, s32[]{:S(2)}) async-start(s8[28311552]{0:T(1024)(128)(4,1)} %bitcast.30), calls=%async_computation.9 | async-start | bytes 8388608
  225.9 56.3 %slice-start.2 = ((s8[28311552]{0:T(1024)(128)(4,1)}), s8[4194304]{0:T(1024)(128)(4,1)S(1)}, s32[]{:S(2)}) async-start(s8[28311552]{0:T(1024)(128)(4,1)} %bitcast.30), calls=%async_computation.10 | async-start | bytes 8388608
  225.9 56.3 %slice-start.3 = ((s8[28311552]{0:T(1024)(128)(4,1)}), s8[4194304]{0:T(1024)(128)(4,1)S(1)}, s32[]{:S(2)}) async-start(s8[28311552]{0:T(1024)(128)(4,1)} %bitcast.30), calls=%async_computation.11 | async-start | bytes 8388608
  225.9 56.3 %slice-start.8 = ((s8[4718592]{0:T(1024)(128)(4,1)}), s8[4194304]{0:T(1024)(128)(4,1)S(1)}, s32[]{:S(2)}) async-start(s8[4718592]{0:T(1024)(128)(4,1)} %bitcast.32), calls=%async_computation.16 | async-start | bytes 8388608
  254.1 28.0 %slice-start.4 = ((s8[28311552]{0:T(1024)(128)(4,1)}), s8[4194304]{0:T(1024)(128)(4,1)S(1)}, s32[]{:S(2)}) async-start(s8[28311552]{0:T(1024)(128)(4,1)} %bitcast.30), calls=%async_computation.12 | async-start | bytes 8388608
  254.1 28.1 %slice-start.5 = ((s8[28311552]{0:T(1024)(128)(4,1)}), s8[4194304]{0:T(1024)(128)(4,1)S(1)}, s32[]{:S(2)}) async-start(s8[28311552]{0:T(1024)(128)(4,1)} %bitcast.30), calls=%async_computation.13 | async-start | bytes 8388608
  254.2 28.1 %slice-start.6 = ((s8[28311552]{0:T(1024)(128)(4,1)}), s8[3145728]{0:T(1024)(128)(4,1)S(1)}, s32[]{:S(2)}) async-start(s8[28311552]{0:T(1024)(128)(4,1)} %bitcast.30), calls=%async_computation.14 | async-start | bytes 6291456
  395.4 47.1 %copy-start.2 = (f32[384,768]{1,0:T(8,128)S(1)}, f32[384,768]{1,0:T(8,128)}, u32[]{:S(2)}) copy-start(f32[384,768]{1,0:T(8,128)} %param.4) | copy-start | bytes 3538948
  395.4 87.1 %all-gather.5.cloned.1.call-start = ((), (), s32[]{:S(2)}) async-start(), calls=%async_computation.5 | async-start | bytes 5898240 | tf_op jit(solution)/shard_map/all_gather | solution.py:16
  445.0 214.4 %all-reduce.5.cloned.1.call-start = ((), (), s32[]{:S(2)}) async-start(), calls=%async_computation.6 | async-start | bytes 9437184 | tf_op jit(solution)/shard_map/psum | solution.py:12
  487.4 380.9 %reduce-scatter.5.cloned.1.call-start = ((), (), s32[]{:S(2)}) async-start(), calls=%async_computation.7 | async-start | bytes 5898240 | tf_op jit(solution)/shard_map/reduce_scatter | solution.py:20
  659.4 27.4 %copy-start = (f32[1536,768]{1,0:T(8,128)S(1)}, f32[1536,768]{1,0:T(8,128)}, u32[]{:S(2)}) copy-start(f32[1536,768]{1,0:T(8,128)} %all-reduce.5.cloned.1.call-done) | copy-start | bytes 14155780
  659.4 54.8 %slice-start.9 = ((s8[4718592]{0:T(1024)(128)(4,1)}), s8[4194304]{0:T(1024)(128)(4,1)S(1)}, s32[]{:S(2)}) async-start(s8[4718592]{0:T(1024)(128)(4,1)} %bitcast.34), calls=%async_computation.17 | async-start | bytes 8388608
  686.8 27.3 %slice-start.10 = ((s8[4718592]{0:T(1024)(128)(4,1)}), s8[524288]{0:T(1024)(128)(4,1)S(1)}, s32[]{:S(2)}) async-start(s8[4718592]{0:T(1024)(128)(4,1)} %bitcast.34), calls=%async_computation.18 | async-start | bytes 1048576
  821.2 47.1 %copy-start.1 = (f32[384,768]{1,0:T(8,128)S(1)}, f32[384,768]{1,0:T(8,128)}, u32[]{:S(2)}) copy-start(f32[384,768]{1,0:T(8,128)} %sub.8) | copy-start | bytes 3538948
Sparse Core Ops, SparseCore 0:
  8.9 40.1 all-gather.2
  54.0 171.8 all-reduce.2
  395.5 46.9 reduce-scatter.2
  445.1 37.4 all-gather.4
  487.5 171.8 all-reduce.4
  821.4 46.9 reduce-scatter.4
where the time goes:
time: 886 us; the launch traced here: 878 us
  waiting for transfers between devices  517 us (58%)
  matrix products  331 us (37%)
  other arithmetic  14.5 us (2%)
  between operations  13.9 us (2%)
    psum x2, waiting for transfers between devices, from_root(): return lax.psum(block, axis)  343 us
    dot_general x6, matrix products, body(): jnp.dot(green * screened[t], columns, precision=lax.Precision.HIGHEST, pr...  166 us
    dot_general x6, matrix products, body(): lax.dot_general(rows * green_weight[t], columns, (((1,), (1,)), ((), ()))...  165 us
    reduce_scatter x2, waiting for transfers between devices, scatter_rows(): lax.psum_scatter(partial_value, 'col', scatter_dimension=0, tiled=True)  94.1 us
    all_gather x2, waiting for transfers between devices, gather_rows(): return lax.all_gather(shard, 'col', axis=0, tiled=True)  79.3 us
  transfers between devices with their start and end apart: 6, of which 6 were waited for; matrix products, arithmetic and copies ran while one was open for 0% of the time, Pallas kernels for 0%

commit v1 on v0

v1 whole, which is shorter than its diff:
```python
import functools

import jax
import jax.numpy as jnp
from jax import lax
from jax.experimental import pallas as pl
from jax.experimental.pallas import tpu as pltpu
from jax.sharding import PartitionSpec as P

PASSES = 2


def split(value):
    high = value.astype(jnp.bfloat16)
    low = (value - high.astype(jnp.float32)).astype(jnp.bfloat16)
    return high, low


def apply_kernel(times, parts, has_total, index_ref, *refs):
    rows_refs, refs = refs[:parts], refs[parts:]
    cols_refs, refs = refs[:parts], refs[parts:]
    weight_ref, screened_ref, refs = refs[0], refs[1], refs[2:]
    total_refs = None
    if has_total:
        total_refs, refs = refs[:parts], refs[parts:]
    out_refs, (weighted, plain) = refs[:parts], refs[parts:]

    @pl.when(pl.program_id(0) == 0)
    def _():
        cols = jnp.concatenate([ref[...] for ref in cols_refs], axis=1)
        width, depth = cols.shape
        high, low = split(cols)
        plain[0:width, :] = high
        plain[width : 2 * width, :] = high
        plain[2 * width : 3 * width, :] = low
        for t in range(times):
            high, low = split((cols * weight_ref[t : t + 1, :]).T)
            weighted[t, 0:depth, :] = high
            weighted[t, depth : 2 * depth, :] = high
            weighted[t, 2 * depth : 3 * depth, :] = low

    high, low = split(jnp.concatenate([ref[...] for ref in rows_refs], axis=1))
    rows = jnp.concatenate([high, low, high], axis=1)
    mixed = None
    for t in range(times):
        green = jnp.dot(rows, weighted[t], preferred_element_type=jnp.float32)
        term = green * screened_ref[t]
        mixed = term if mixed is None else mixed + term
    high, low = split(mixed)
    mixed = jnp.concatenate([high, low, high], axis=1)
    applied = jnp.dot(mixed, plain[...], preferred_element_type=jnp.float32)
    part = applied.shape[1] // parts
    for k in range(parts):
        value = applied[:, k * part : (k + 1) * part]
        out_refs[k][...] = value + total_refs[k][...] if has_total else value


def apply_block(index, rows, cols, weight, screened, total):
    times = screened.shape[0]
    parts = len(rows)
    n_rows, part = rows[0].shape
    depth = parts * part
    width = cols[0].shape[0]
    tile = next(k for k in (512, 384, 256, 128, n_rows) if n_rows % k == 0)
    row_spec = pl.BlockSpec((tile, part), lambda i, ix: (i, 0))
    in_specs = [row_spec] * parts
    in_specs += [pl.BlockSpec((width, part), lambda i, ix: (0, 0))] * parts
    in_specs += [
        pl.BlockSpec((times, depth), lambda i, ix: (0, 0)),
        pl.BlockSpec((times, tile, width), lambda i, ix: (0, i, ix[0])),
    ]
    args = [index, *rows, *cols, weight, screened]
    if total is not None:
        in_specs += [row_spec] * parts
        args += total
    return pl.pallas_call(
        functools.partial(apply_kernel, times, parts, total is not None),
        out_shape=[jax.ShapeDtypeStruct((n_rows, part), jnp.float32)] * parts,
        grid_spec=pltpu.PrefetchScalarGridSpec(
            num_scalar_prefetch=1,
            grid=(n_rows // tile,),
            in_specs=in_specs,
            out_specs=[row_spec] * parts,
            scratch_shapes=[
                pltpu.VMEM((times, 3 * depth, width), jnp.bfloat16),
                pltpu.VMEM((3 * width, depth), jnp.bfloat16),
            ],
        ),
        compiler_params=pltpu.CompilerParams(
            dimension_semantics=("arbitrary",), vmem_limit_bytes=56 * 1024 * 1024
        ),
        cost_estimate=pl.CostEstimate(
            flops=6 * (times + 1) * n_rows * width * depth,
            bytes_accessed=4 * (times * n_rows * width + 3 * n_rows * depth),
            transcendentals=0,
        ),
    )(*args)


def scatter_rows(value):
    n_col = lax.axis_size("col")
    if n_col & (n_col - 1):
        return lax.psum_scatter(value, "col", scatter_dimension=0, tiled=True)
    me = lax.axis_index("col")
    points = value.shape[0] // n_col
    value = value.reshape(n_col, points, value.shape[1])
    distance = 1
    while distance < n_col:
        bit = (me // distance) % 2
        pairs = value.reshape((value.shape[0] // 2, 2) + value.shape[1:])
        mine = lax.dynamic_index_in_dim(pairs, bit, 1, keepdims=False)
        theirs = lax.dynamic_index_in_dim(pairs, 1 - bit, 1, keepdims=False)
        swap = [(k, k ^ distance) for k in range(n_col)]
        value = mine + lax.ppermute(theirs, "col", swap)
        distance *= 2
    return value[0]


def body(orbitals, screened, green_weight, time_weight):
    n_row = lax.axis_size("row")
    n_col = lax.axis_size("col")
    factor = n_col // n_row
    points, depth = orbitals.shape
    weight = green_weight * time_weight[:, None]
    to_columns = [
        ((c // factor) * n_col + (c % factor) * n_row + m, m * n_col + c)
        for m in range(n_row)
        for c in range(n_col)
    ]
    ring = [(k, (k + 1) % n_row) for k in range(n_row)]
    me = lax.axis_index("row")
    parts = 1
    own = jnp.split(orbitals, parts, axis=1)
    for step in range(PASSES):
        piece = [lax.ppermute(o, ("row", "col"), to_columns) for o in own]
        rows = [lax.all_gather(o, "col", axis=0, tiled=True) for o in own]
        total = None
        if points % 128 == 0:
            for hop in range(n_row):
                later = None
                if hop < n_row - 1:
                    if total is not None:
                        piece, total = lax.optimization_barrier((piece, total))
                    later = [lax.ppermute(p, "row", ring) for p in piece]
                index = lax.rem(me - hop + n_row, n_row).astype(jnp.int32).reshape(1)
                total = apply_block(index, rows, piece, weight, screened, total)
                piece = later
        else:
            columns = [lax.all_gather(p, "row", axis=0, tiled=True) for p in piece]
            index = jnp.zeros((1,), jnp.int32)
            total = apply_block(index, rows, columns, weight, screened, None)
        own = [
            o - scatter_rows(v)
            for o, v in zip(own, total)
        ]
    return jnp.concatenate(own, axis=1)


def solution(mesh):
    in_specs = (P(("snap", "row", "col"), None), P("snap", "row", "col"), P("snap", None), P())
    out_specs = P(("snap", "row", "col"), None)
    return jax.shard_map(body, mesh=mesh, in_specs=in_specs, out_specs=out_specs, check_vma=False)
```

time: 886 us -> 470 us (0.53)
  waiting for transfers between devices: 517 us -> 127 us
  matrix products: 331 us -> 0 us
  Pallas kernels: 0 us -> 170 us
  starting transfers between devices: 0.21 us -> 134 us
    psum x2 -> x0, waiting for transfers between devices: 343 us -> none  [from_root(): return lax.psum(block, axis)]
    dot_general x12 -> x0, matrix products: 331 us -> none  [the longest x6 166 us: body(): jnp.dot(green * screened[t], columns, precision=lax.Precision.HIGHEST, pr...]
    pallas_call x0 -> x8, Pallas kernels: none -> 170 us  [apply_block(): pl.pallas_call(functools.partial(apply_kernel, times, parts, total is not...]
    ppermute x0 -> x12, starting transfers between devices: none -> 134 us  [the longest x6 130 us: body(): later = [lax.ppermute(p, 'row', ring) for p in piece]]
    reduce_scatter x2 -> x0, waiting for transfers between devices: 94.1 us -> none  [scatter_rows(): lax.psum_scatter(partial_value, 'col', scatter_dimension=0, tiled=True)]
    ppermute x0 -> x12, waiting for transfers between devices: none -> 88.9 us  [the longest x4 65.4 us: scatter_rows(): value = mine + lax.ppermute(theirs, 'col', swap)]
    all_gather x2, waiting for transfers between devices: 79.3 us -> 37.2 us  [body(): rows = [lax.all_gather(o, 'col', axis=0, tiled=True) for o in own]]
    select_n x2 -> x0, other arithmetic: 9.63 us -> none  [from_root(): jnp.where(lax.axis_index(axis) == owner, block, jnp.zeros_like(block))]
  transfers between devices with their start and end apart: 6 -> 14, of which waited for: 6 -> 10; matrix products, arithmetic and copies ran while one was open for 0% -> 0% of each run, Pallas kernels for 0% -> 28%
where the time goes in v1:
time: 470 us; the launch traced here: 462 us
  Pallas kernels  170 us (36%)
  starting transfers between devices  134 us (29%)
  waiting for transfers between devices  127 us (27%)
  between operations  14 us (3%)
  local copies, waits for them, and re-layouts  8.65 us (2%)
  other arithmetic  8.12 us (2%)
    pallas_call x8, Pallas kernels, apply_block(): pl.pallas_call(functools.partial(apply_kernel, times, parts, total is not...  170 us
    ppermute x6, starting transfers between devices, body(): later = [lax.ppermute(p, 'row', ring) for p in piece]  130 us
    ppermute x4, waiting for transfers between devices, scatter_rows(): value = mine + lax.ppermute(theirs, 'col', swap)  65.4 us
    all_gather x2, waiting for transfers between devices, body(): rows = [lax.all_gather(o, 'col', axis=0, tiled=True) for o in own]  37.2 us
    ppermute x6, waiting for transfers between devices, body(): later = [lax.ppermute(p, 'row', ring) for p in piece]  23.5 us
  transfers between devices with their start and end apart: 14, of which 10 were waited for; matrix products, arithmetic and copies ran while one was open for 0% of the time, Pallas kernels for 28%

profile of v1, /device:TPU:0, one launch (start us, length us, event | category | flops | bytes accessed | tf_op | source)
XLA Modules:
  0.0 462.0 jit_solution(7167257660921477261)
XLA Ops:
  6.5 0.7 all-gather.3.cloned.1.call-update
  7.3 0.0 all-gather.5.cloned.1.call-start
  7.3 1.9 collective-permute-start
  9.2 26.9 %collective-permute-start.1 = (f32[384,768]{1,0:T(8,128)S(1)}, f32[384,768]{1,0:T(8,128)S(1)}, u32[]{:S(2)}, u32[]{:S(2)}) collective-permute-start(f32[384,768]{1,0:T(8,128)S(1)} %collective-permute-done.refs_1_), channel_id=1, source_target_pairs={{0,4},{4,8},{8,12},{12,0},{1,5},{5,9},{9,13},{13,1},{2,6},{6,10},{... | collective-permute-start | bytes 3538952 | tf_op jit(solution)/shard_map/ppermute | solution.py:144
  36.1 1.4 broadcast_multiply_fusion.refs_2_
  37.5 21.1 %all-gather.3.cloned.1.call-done.refs_0_ = f32[1536,768]{1,0:T(8,128)} async-done(((f32[384,768]{1,0:T(8,128)}), f32[1536,768]{1,0:T(8,128)}) %all-gather.3.cloned.1.call-update) | async-done | bytes 4718608 | tf_op jit(solution)/shard_map/all_gather | solution.py:136
  58.6 20.9 %shard_map.46.refs_4_ = f32[1536,768]{1,0:T(8,128)} custom-call(s32[1]{0:T(128)} %bitcast.1.index_ref, f32[1536,768]{1,0:T(8,128)} %all-gather.3.cloned.1.call-done.refs_0_, f32[384,768]{1,0:T(8,128)} %copy-done.9, f32[3,768]{1,0:T(4,128)} %broadcast_multiply_fusion.refs_2_, f32[3,1536,1536]{2,1,0:T(8,128)} %refs_3_.15), custom_call_target="tpu_custom_call" | custom-call | flops 10871635968 | bytes 21233664 | tf_op jit(solution)/shard_map/pallas_call | solution.py:76
  79.5 37.5 %collective-permute-start.2 = (f32[384,768]{1,0:T(8,128)S(1)}, f32[384,768]{1,0:T(8,128)S(1)}, u32[]{:S(2)}, u32[]{:S(2)}) collective-permute-start(f32[384,768]{1,0:T(8,128)S(1)} %collective-permute-done.1.refs_1_), channel_id=1, source_target_pairs={{0,4},{4,8},{8,12},{12,0},{1,5},{5,9},{9,13},{13,1},{2,6},{6,10},{... | collective-permute-start | bytes 3538952 | tf_op jit(solution)/shard_map/ppermute | solution.py:144
  116.9 21.4 %shard_map.47.refs_4_ = f32[1536,768]{1,0:T(8,128)} custom-call(s32[1]{0:T(128)} %bitcast.2.index_ref, f32[1536,768]{1,0:T(8,128)} %all-gather.3.cloned.1.call-done.refs_0_, f32[384,768]{1,0:T(8,128)} %copy-done.5, f32[3,768]{1,0:T(4,128)} %broadcast_multiply_fusion.refs_2_, f32[3,1536,1536]{2,1,0:T(8,128)} %refs_3_.15, f32[1536,768]{1,0:T(8,128)} %shard_map.46.refs_4_), custom_call_target="tpu_custom_call" | custom-call | flops 10871635968 | bytes 21233664 | tf_op jit(solution)/shard_map/pallas_call | solution.py:76
  138.4 5.4 %collective-permute-done.2.refs_1_ = f32[384,768]{1,0:T(8,128)S(1)} collective-permute-done((f32[384,768]{1,0:T(8,128)S(1)}, f32[384,768]{1,0:T(8,128)S(1)}, u32[]{:S(2)}, u32[]{:S(2)}) %collective-permute-start.2) | collective-permute-done | bytes 1179680 | tf_op jit(solution)/shard_map/ppermute | solution.py:144
  143.8 0.2 collective-permute-start.3
  144.0 0.8 copy-done.3
  144.8 21.3 %shard_map.48.refs_4_ = f32[1536,768]{1,0:T(8,128)} custom-call(s32[1]{0:T(128)} %bitcast.3.index_ref, f32[1536,768]{1,0:T(8,128)} %all-gather.3.cloned.1.call-done.refs_0_, f32[384,768]{1,0:T(8,128)} %copy-done.3, f32[3,768]{1,0:T(4,128)} %broadcast_multiply_fusion.refs_2_, f32[3,1536,1536]{2,1,0:T(8,128)} %refs_3_.15, f32[1536,768]{1,0:T(8,128)} %shard_map.47.refs_4_), custom_call_target="tpu_custom_call" | custom-call | flops 10871635968 | bytes 21233664 | tf_op jit(solution)/shard_map/pallas_call | solution.py:76
  166.2 6.0 %collective-permute-done.3.refs_1_ = f32[384,768]{1,0:T(8,128)S(1)} collective-permute-done((f32[384,768]{1,0:T(8,128)S(1)}, f32[384,768]{1,0:T(8,128)S(1)}, u32[]{:S(2)}, u32[]{:S(2)}) %collective-permute-start.3) | collective-permute-done | bytes 1179680 | tf_op jit(solution)/shard_map/ppermute | solution.py:144
  172.2 1.0 copy-done.4
  173.2 21.4 %shard_map.49 = f32[1536,768]{1,0:T(8,128)} custom-call(s32[1]{0:T(128)} %bitcast.index_ref, f32[1536,768]{1,0:T(8,128)} %all-gather.3.cloned.1.call-done.refs_0_, f32[384,768]{1,0:T(8,128)} %copy-done.4, f32[3,768]{1,0:T(4,128)} %broadcast_multiply_fusion.refs_2_, f32[3,1536,1536]{2,1,0:T(8,128)} %refs_3_.15, f32[1536,768]{1,0:T(8,128)} %shard_map.48.refs_4_), custom_call_target="tpu_custom_call" | custom-call | flops 10871635968 | bytes 21233664 | tf_op jit(solution)/shard_map/pallas_call | solution.py:76
  194.6 1.8 dynamic-slice_bitcast_fusion.1
  196.4 0.1 collective-permute-start.4
  196.5 4.6 collective-permute-done.4
  201.1 2.7 bitcast_add_fusion.1
  203.8 0.0 copy-start.2
  203.8 1.1 constant_dynamic-slice_fusion.1
  204.9 0.0 collective-permute-start.5
  204.9 28.3 %collective-permute-done.5 = f32[1,384,768]{2,1,0:T(8,128)} collective-permute-done((f32[1,384,768]{2,1,0:T(8,128)}, f32[1,384,768]{2,1,0:T(8,128)}, u32[]{:S(2)}, u32[]{:S(2)}) %collective-permute-start.5) | collective-permute-done | bytes 1179680 | tf_op jit(solution)/shard_map/ppermute | solution.py:114
  233.3 2.5 bitcast_subtract_fusion.1
  235.8 0.0 all-gather.5.cloned.1.call-update
  235.8 1.9 collective-permute-start.6
  237.7 29.2 %collective-permute-start.7 = (f32[384,768]{1,0:T(8,128)S(1)}, f32[384,768]{1,0:T(8,128)S(1)}, u32[]{:S(2)}, u32[]{:S(2)}) collective-permute-start(f32[384,768]{1,0:T(8,128)S(1)} %collective-permute-done.6.refs_1_), channel_id=1, source_target_pairs={{0,4},{4,8},{8,12},{12,0},{1,5},{5,9},{9,13},{13,1},{2,6},{6,10},{... | collective-permute-start | bytes 3538952 | tf_op jit(solution)/shard_map/ppermute | solution.py:144
  266.9 16.1 %all-gather.5.cloned.1.call-done.refs_0_ = f32[1536,768]{1,0:T(8,128)} async-done(((f32[384,768]{1,0:T(8,128)}), f32[1536,768]{1,0:T(8,128)}) %all-gather.5.cloned.1.call-update) | async-done | bytes 4718608 | tf_op jit(solution)/shard_map/all_gather | solution.py:136
  283.0 21.0 %shard_map.50.refs_4_ = f32[1536,768]{1,0:T(8,128)} custom-call(s32[1]{0:T(128)} %bitcast.1.index_ref, f32[1536,768]{1,0:T(8,128)} %all-gather.5.cloned.1.call-done.refs_0_, f32[384,768]{1,0:T(8,128)} %copy-done.10, f32[3,768]{1,0:T(4,128)} %broadcast_multiply_fusion.refs_2_, f32[3,1536,1536]{2,1,0:T(8,128)} %refs_3_.15), custom_call_target="tpu_custom_call" | custom-call | flops 10871635968 | bytes 21233664 | tf_op jit(solution)/shard_map/pallas_call | solution.py:76
  304.0 36.2 %collective-permute-start.8 = (f32[384,768]{1,0:T(8,128)S(1)}, f32[384,768]{1,0:T(8,128)S(1)}, u32[]{:S(2)}, u32[]{:S(2)}) collective-permute-start(f32[384,768]{1,0:T(8,128)S(1)} %collective-permute-done.7.refs_1_), channel_id=1, source_target_pairs={{0,4},{4,8},{8,12},{12,0},{1,5},{5,9},{9,13},{13,1},{2,6},{6,10},{... | collective-permute-start | bytes 3538952 | tf_op jit(solution)/shard_map/ppermute | solution.py:144
  340.2 21.3 %shard_map.51.refs_4_ = f32[1536,768]{1,0:T(8,128)} custom-call(s32[1]{0:T(128)} %bitcast.2.index_ref, f32[1536,768]{1,0:T(8,128)} %all-gather.5.cloned.1.call-done.refs_0_, f32[384,768]{1,0:T(8,128)} %copy-done.6, f32[3,768]{1,0:T(4,128)} %broadcast_multiply_fusion.refs_2_, f32[3,1536,1536]{2,1,0:T(8,128)} %refs_3_.15, f32[1536,768]{1,0:T(8,128)} %shard_map.50.refs_4_), custom_call_target="tpu_custom_call" | custom-call | flops 10871635968 | bytes 21233664 | tf_op jit(solution)/shard_map/pallas_call | solution.py:76
  361.5 5.8 %collective-permute-done.8.refs_1_ = f32[384,768]{1,0:T(8,128)S(1)} collective-permute-done((f32[384,768]{1,0:T(8,128)S(1)}, f32[384,768]{1,0:T(8,128)S(1)}, u32[]{:S(2)}, u32[]{:S(2)}) %collective-permute-start.8) | collective-permute-done | bytes 1179680 | tf_op jit(solution)/shard_map/ppermute | solution.py:144
  367.3 0.2 collective-permute-start.9
  367.5 0.8 copy-done.7
  368.3 21.4 %shard_map.52.refs_4_ = f32[1536,768]{1,0:T(8,128)} custom-call(s32[1]{0:T(128)} %bitcast.3.index_ref, f32[1536,768]{1,0:T(8,128)} %all-gather.5.cloned.1.call-done.refs_0_, f32[384,768]{1,0:T(8,128)} %copy-done.7, f32[3,768]{1,0:T(4,128)} %broadcast_multiply_fusion.refs_2_, f32[3,1536,1536]{2,1,0:T(8,128)} %refs_3_.15, f32[1536,768]{1,0:T(8,128)} %shard_map.51.refs_4_), custom_call_target="tpu_custom_call" | custom-call | flops 10871635968 | bytes 21233664 | tf_op jit(solution)/shard_map/pallas_call | solution.py:76
  389.8 6.2 %collective-permute-done.9.refs_1_ = f32[384,768]{1,0:T(8,128)S(1)} collective-permute-done((f32[384,768]{1,0:T(8,128)S(1)}, f32[384,768]{1,0:T(8,128)S(1)}, u32[]{:S(2)}, u32[]{:S(2)}) %collective-permute-start.9) | collective-permute-done | bytes 1179680 | tf_op jit(solution)/shard_map/ppermute | solution.py:144
  396.0 1.0 copy-done.8
  397.0 21.3 %shard_map.53 = f32[1536,768]{1,0:T(8,128)} custom-call(s32[1]{0:T(128)} %bitcast.index_ref, f32[1536,768]{1,0:T(8,128)} %all-gather.5.cloned.1.call-done.refs_0_, f32[384,768]{1,0:T(8,128)} %copy-done.8, f32[3,768]{1,0:T(4,128)} %broadcast_multiply_fusion.refs_2_, f32[3,1536,1536]{2,1,0:T(8,128)} %refs_3_.15, f32[1536,768]{1,0:T(8,128)} %shard_map.52.refs_4_), custom_call_target="tpu_custom_call" | custom-call | flops 10871635968 | bytes 21233664 | tf_op jit(solution)/shard_map/pallas_call | solution.py:76
  418.4 2.0 dynamic-slice_bitcast_fusion
  420.3 0.1 collective-permute-start.10
  420.4 4.5 collective-permute-done.10
  424.9 0.3 bitcast_add_fusion
  425.2 0.0 copy-start.1
  425.2 0.1 constant_dynamic-slice_fusion
  425.3 0.1 collective-permute-start.11
  425.4 28.0 %collective-permute-done.11 = f32[1,384,768]{2,1,0:T(8,128)S(1)} collective-permute-done((f32[1,384,768]{2,1,0:T(8,128)S(1)}, f32[1,384,768]{2,1,0:T(8,128)S(1)}, u32[]{:S(2)}, u32[]{:S(2)}) %collective-permute-start.11) | collective-permute-done | bytes 1179680 | tf_op jit(solution)/shard_map/ppermute | solution.py:114
  453.4 1.3 bitcast_subtract_fusion
  (21 shorter events, 0.0 us)
Async XLA Ops:
  6.5 52.1 %all-gather.3.cloned.1.call-start = ((), (), s32[]{:S(2)}) async-start(), calls=%async_computation | async-start | bytes 5898240 | tf_op jit(solution)/shard_map/all_gather | solution.py:136
  7.3 275.7 %all-gather.5.cloned.1.call-start = ((), (), s32[]{:S(2)}) async-start(), calls=%async_computation.1 | async-start | bytes 5898240 | tf_op jit(solution)/shard_map/all_gather | solution.py:136
  7.3 1.9 collective-permute-start
  9.2 49.4 %copy-start.9 = (f32[384,768]{1,0:T(8,128)}, f32[384,768]{1,0:T(8,128)S(1)}, u32[]{:S(2)}) copy-start(f32[384,768]{1,0:T(8,128)S(1)} %collective-permute-done.refs_1_) | copy-start | bytes 3538948
  9.2 70.2 %collective-permute-start.1 = (f32[384,768]{1,0:T(8,128)S(1)}, f32[384,768]{1,0:T(8,128)S(1)}, u32[]{:S(2)}, u32[]{:S(2)}) collective-permute-start(f32[384,768]{1,0:T(8,128)S(1)} %collective-permute-done.refs_1_), channel_id=1, source_target_pairs={{0,4},{4,8},{8,12},{12,0},{1,5},{5,9},{9,13},{13,1},{2,6},{6,10},{... | collective-permute-start | bytes 3538952 | tf_op jit(solution)/shard_map/ppermute | solution.py:144
  79.5 37.5 %copy-start.5 = (f32[384,768]{1,0:T(8,128)}, f32[384,768]{1,0:T(8,128)S(1)}, u32[]{:S(2)}) copy-start(f32[384,768]{1,0:T(8,128)S(1)} %collective-permute-done.1.refs_1_) | copy-start | bytes 3538948
  79.5 64.3 %collective-permute-start.2 = (f32[384,768]{1,0:T(8,128)S(1)}, f32[384,768]{1,0:T(8,128)S(1)}, u32[]{:S(2)}, u32[]{:S(2)}) collective-permute-start(f32[384,768]{1,0:T(8,128)S(1)} %collective-permute-done.1.refs_1_), channel_id=1, source_target_pairs={{0,4},{4,8},{8,12},{12,0},{1,5},{5,9},{9,13},{13,1},{2,6},{6,10},{... | collective-permute-start | bytes 3538952 | tf_op jit(solution)/shard_map/ppermute | solution.py:144
  143.8 1.0 copy-start.3
  143.8 28.3 %collective-permute-start.3 = (f32[384,768]{1,0:T(8,128)S(1)}, f32[384,768]{1,0:T(8,128)S(1)}, u32[]{:S(2)}, u32[]{:S(2)}) collective-permute-start(f32[384,768]{1,0:T(8,128)S(1)} %collective-permute-done.2.refs_1_), channel_id=1, source_target_pairs={{0,4},{4,8},{8,12},{12,0},{1,5},{5,9},{9,13},{13,1},{2,6},{6,10},{... | collective-permute-start | bytes 3538952 | tf_op jit(solution)/shard_map/ppermute | solution.py:144
  172.2 1.0 copy-start.4
  196.4 4.7 %collective-permute-start.4 = (f32[2,384,768]{2,1,0:T(8,128)S(1)}, f32[2,384,768]{2,1,0:T(8,128)}, u32[]{:S(2)}, u32[]{:S(2)}) collective-permute-start(f32[2,384,768]{2,1,0:T(8,128)S(1)} %dynamic-slice_bitcast_fusion.1), channel_id=1, source_target_pairs={{0,1},{1,0},{2,3},{3,2},{4,5},{5,4},{6,7},{7,6},{8,9},{9,8},{10,11... | collective-permute-start | bytes 7077896 | tf_op jit(solution)/shard_map/ppermute | solution.py:114
  203.8 29.4 %copy-start.2 = (f32[384,768]{1,0:T(8,128)S(1)}, f32[384,768]{1,0:T(8,128)}, u32[]{:S(2)}) copy-start(f32[384,768]{1,0:T(8,128)} %param.4) | copy-start | bytes 3538948
  204.9 28.3 %collective-permute-start.5 = (f32[1,384,768]{2,1,0:T(8,128)}, f32[1,384,768]{2,1,0:T(8,128)}, u32[]{:S(2)}, u32[]{:S(2)}) collective-permute-start(f32[1,384,768]{2,1,0:T(8,128)} %constant_dynamic-slice_fusion.1), channel_id=1, source_target_pairs={{0,2},{1,3},{2,0},{3,1},{4,6},{5,7},{6,4},{7,5},{8,10},{9,11},{10,... | collective-permute-start | bytes 3538952 | tf_op jit(solution)/shard_map/ppermute | solution.py:114
  235.8 1.9 collective-permute-start.6
  237.7 45.3 %copy-start.10 = (f32[384,768]{1,0:T(8,128)}, f32[384,768]{1,0:T(8,128)S(1)}, u32[]{:S(2)}) copy-start(f32[384,768]{1,0:T(8,128)S(1)} %collective-permute-done.6.refs_1_) | copy-start | bytes 3538948
  237.7 66.2 %collective-permute-start.7 = (f32[384,768]{1,0:T(8,128)S(1)}, f32[384,768]{1,0:T(8,128)S(1)}, u32[]{:S(2)}, u32[]{:S(2)}) collective-permute-start(f32[384,768]{1,0:T(8,128)S(1)} %collective-permute-done.6.refs_1_), channel_id=1, source_target_pairs={{0,4},{4,8},{8,12},{12,0},{1,5},{5,9},{9,13},{13,1},{2,6},{6,10},{... | collective-permute-start | bytes 3538952 | tf_op jit(solution)/shard_map/ppermute | solution.py:144
  303.9 36.2 %copy-start.6 = (f32[384,768]{1,0:T(8,128)}, f32[384,768]{1,0:T(8,128)S(1)}, u32[]{:S(2)}) copy-start(f32[384,768]{1,0:T(8,128)S(1)} %collective-permute-done.7.refs_1_) | copy-start | bytes 3538948
  304.0 63.3 %collective-permute-start.8 = (f32[384,768]{1,0:T(8,128)S(1)}, f32[384,768]{1,0:T(8,128)S(1)}, u32[]{:S(2)}, u32[]{:S(2)}) collective-permute-start(f32[384,768]{1,0:T(8,128)S(1)} %collective-permute-done.7.refs_1_), channel_id=1, source_target_pairs={{0,4},{4,8},{8,12},{12,0},{1,5},{5,9},{9,13},{13,1},{2,6},{6,10},{... | collective-permute-start | bytes 3538952 | tf_op jit(solution)/shard_map/ppermute | solution.py:144
  367.3 1.0 copy-start.7
  367.3 28.7 %collective-permute-start.9 = (f32[384,768]{1,0:T(8,128)S(1)}, f32[384,768]{1,0:T(8,128)S(1)}, u32[]{:S(2)}, u32[]{:S(2)}) collective-permute-start(f32[384,768]{1,0:T(8,128)S(1)} %collective-permute-done.8.refs_1_), channel_id=1, source_target_pairs={{0,4},{4,8},{8,12},{12,0},{1,5},{5,9},{9,13},{13,1},{2,6},{6,10},{... | collective-permute-start | bytes 3538952 | tf_op jit(solution)/shard_map/ppermute | solution.py:144
  396.0 1.0 copy-start.8
  418.4 6.6 %copy-start = (f32[1536,768]{1,0:T(8,128)S(1)}, f32[1536,768]{1,0:T(8,128)}, u32[]{:S(2)}) copy-start(f32[1536,768]{1,0:T(8,128)} %shard_map.53) | copy-start | bytes 14155780
  420.3 4.6 collective-permute-start.10
  425.2 28.2 %copy-start.1 = (f32[384,768]{1,0:T(8,128)S(1)}, f32[384,768]{1,0:T(8,128)}, u32[]{:S(2)}) copy-start(f32[384,768]{1,0:T(8,128)} %bitcast_subtract_fusion.1) | copy-start | bytes 3538948
  425.3 28.1 %collective-permute-start.11 = (f32[1,384,768]{2,1,0:T(8,128)S(1)}, f32[1,384,768]{2,1,0:T(8,128)S(1)}, u32[]{:S(2)}, u32[]{:S(2)}) collective-permute-start(f32[1,384,768]{2,1,0:T(8,128)S(1)} %constant_dynamic-slice_fusion), channel_id=1, source_target_pairs={{0,2},{1,3},{2,0},{3,1},{4,6},{5,7},{6,4},{7,5},{8,10},{9,11},{10,... | collective-permute-start | bytes 3538952 | tf_op jit(solution)/shard_map/ppermute | solution.py:114
Sparse Core Ops, SparseCore 0:
  8.9 49.6 all-gather.2
  235.9 47.0 all-gather.4
